TPU v7x, 512 devices: a whole 4x8x8 slice. The times are simulated.
512 devices in a mesh: pipe: 8 (over z), ctx: 32 (over x, y_hi, core), tp: 2 (over y_lo).
Axes of the slice: x: 4, y: 8 (y_hi: 4, y_lo: 2; y = y_hi * 2 + y_lo), z: 8, core: 2. Of those that a mesh axis runs over, the one named last changes fastest.
Arguments:
- queries: bfloat16 [8, 2048, 128, 128], P('pipe', 'ctx', 'tp'), may hold values from -10 to 10
- span_keys: bfloat16 [8, 2048, 8, 128], P('pipe', 'ctx', 'tp'), may hold values from -6 to 6
- span_values: bfloat16 [8, 2048, 8, 128], P('pipe', 'ctx', 'tp'), may hold values from -12 to 12
- cache_keys: bfloat16 [8, 1024, 8, 128], P('pipe', 'ctx', 'tp'), may hold values from -6 to 6
- cache_values: bfloat16 [8, 1024, 8, 128], P('pipe', 'ctx', 'tp'), may hold values from -6 to 6
- scale_exps: int32 [8, 64, 8, 2], P('pipe', 'ctx', 'tp'), may hold values from -3 to 1
- block_order: int32 [8, 64], P('pipe'), may hold values from 0 to 63, each once within a row
Outputs:
- handed: bfloat16 [8, 2048, 128, 128], P('pipe', 'ctx', 'tp')
All inputs are finite; a program needn't handle non-finite values.
Results may differ from a plain program's by a relative error of at most 0.006.
Values may be sent and summed in bfloat16 or wider, within the bound.
No kernel may reach another device: no remote copies, remote signals or barrier semaphores. Data moves between devices by JAX's collectives and lax.ppermute only.
A program may use at most 128 MiB of HBM per device.

v0:
```python
import jax
import jax.numpy as jnp
from jax import lax
from jax.sharding import PartitionSpec as P

CBLK = 16


def shifted(value, axis, steps):
    count = lax.axis_size(axis)
    pairs = [(source, (source + steps) % count) for source in range(count)]
    return lax.ppermute(value, axis, pairs)


def hadamard(order):
    rows = jnp.arange(order, dtype=jnp.int32)[:, None]
    cols = jnp.arange(order, dtype=jnp.int32)[None, :]
    common = jnp.zeros((order, order), jnp.int32)
    for bit in range(order.bit_length() - 1):
        common = common + (jnp.right_shift(rows, bit) & 1) * (jnp.right_shift(cols, bit) & 1)
    signs = 1.0 - 2.0 * (common % 2).astype(jnp.float32)
    return signs * (1.0 / order**0.5)


def table_lookup(table, slots):
    match = jnp.arange(table.shape[0], dtype=jnp.int32)[None, :] == slots[:, None]
    return jnp.sum(jnp.where(match, table[None, :], 0), axis=1)


def attend(carry, block, grouped, pos_query, order, half, cache_len, rows_dev):
    best, total, accum = carry
    keys = block[:, :, 0, :]
    vals = block[:, :, 1, :]
    count = block.shape[0]
    global_row = jnp.arange(count, dtype=jnp.int32)
    owner = global_row // rows_dev
    local = global_row % rows_dev
    offset = jnp.maximum(local - cache_len, 0)
    pos_key = table_lookup(order, 2 * owner + offset // half) * half + offset % half
    visible = (local < cache_len)[None, :] | (pos_key[None, :] <= pos_query[:, None])
    inv = 1.0 / grouped.shape[-1] ** 0.5
    score = jnp.einsum("tgqd,kgd->gqtk", grouped, keys, preferred_element_type=jnp.float32) * inv
    score = jnp.where(visible[None, None], score, -jnp.inf)
    best_new = jnp.max(score, axis=-1)
    safe = jnp.where(best_new == -jnp.inf, 0.0, best_new)
    expo = jnp.exp(score - safe[..., None])
    rescale = jnp.exp(best - safe)
    total = total * rescale + jnp.sum(expo, axis=-1)
    accum = accum * rescale[..., None] + jnp.einsum(
        "gqtk,kgd->gqtd", expo.astype(jnp.bfloat16), vals, preferred_element_type=jnp.float32
    )
    return (best_new, total, accum)


def on_device(queries, span_keys, span_values, cache_keys, cache_values, scale_exps, block_order):
    mine = lax.axis_index("ctx")
    tok_local = queries.shape[1]
    head_local = queries.shape[2]
    kv_local = span_keys.shape[2]
    width = queries.shape[3]
    cache_len = cache_keys.shape[1]
    half = tok_local // 2
    rows_dev = cache_len + tok_local
    grouped = queries[0].reshape(tok_local, kv_local, head_local // kv_local, width)
    order = block_order[0]
    factor = jnp.repeat(jnp.exp2(scale_exps[0].astype(jnp.float32)), CBLK, axis=0)
    keys_ctx = (cache_keys[0].astype(jnp.float32) * factor[:, :, 0:1]).astype(jnp.bfloat16)
    vals_ctx = (cache_values[0].astype(jnp.float32) * factor[:, :, 1:2]).astype(jnp.bfloat16)
    own_keys = jnp.concatenate([keys_ctx, span_keys[0]], axis=0)
    own_vals = jnp.concatenate([vals_ctx, span_values[0]], axis=0)
    own_block = jnp.stack([own_keys, own_vals], axis=2)
    index = jnp.arange(tok_local, dtype=jnp.int32)
    pos_query = table_lookup(order, 2 * mine + index // half) * half + index % half
    group_size = head_local // kv_local
    initial = (
        jnp.full((kv_local, group_size, tok_local), -jnp.inf, jnp.float32),
        jnp.zeros((kv_local, group_size, tok_local), jnp.float32),
        jnp.zeros((kv_local, group_size, tok_local, width), jnp.float32),
    )
    carry = attend(
        initial,
        lax.all_gather(own_block, "ctx", axis=0, tiled=True),
        grouped,
        pos_query,
        order,
        half,
        cache_len,
        rows_dev,
    )
    best, total, accum = carry
    mixed = accum / total[..., None]
    rotated = jnp.dot(mixed.reshape(-1, width), hadamard(width))
    rotated = rotated.reshape(kv_local, group_size, tok_local, width).transpose(2, 0, 1, 3)
    result = rotated.reshape(1, tok_local, head_local, width).astype(jnp.bfloat16)
    return shifted(result, "pipe", 1)


def solution(mesh):
    placed = (
        P("pipe", "ctx", "tp", None),
        P("pipe", "ctx", "tp", None),
        P("pipe", "ctx", "tp", None),
        P("pipe", "ctx", "tp", None),
        P("pipe", "ctx", "tp", None),
        P("pipe", "ctx", "tp", None),
        P("pipe", None),
    )
    return jax.shard_map(
        on_device,
        mesh=mesh,
        in_specs=placed,
        out_specs=P("pipe", "ctx", "tp", None),
        check_vma=False,
    )
```

profile of v0, /device:TPU:1, one launch (start us, length us, event | category | flops | bytes accessed | tf_op | source)
XLA Modules:
  0.0 190.2 jit_solution(14502393834735405781)
XLA Ops:
  6.5 0.0 copy-start
  6.5 0.0 all-gather.2.cloned.1.call-start
  6.5 0.8 exponential_bitcast_fusion
  7.3 0.1 copy.16
  7.4 0.1 broadcast_in_dim.66
  7.5 0.1 reshape.263
  7.6 0.9 copy.34
  8.4 0.9 copy.33
  9.3 0.9 fusion.29
  10.2 0.7 pad_maximum_fusion
  10.9 0.0 all-gather.2.cloned.1.call-update
  11.0 0.8 select_reduce_fusion.1
  11.9 0.9 select_reduce_fusion
  12.8 0.2 compare_or_fusion
  13.0 78.2 %all-gather.2.cloned.1.call-done = bf16[3072,4,2,128]{3,0,1,2:T(8,128)(2,1)} async-done(((bf16[96,4,2,128]{3,0,1,2:T(8,128)(2,1)}), bf16[3072,4,2,128]{3,0,1,2:T(8,128)(2,1)}) %all-gather.2.cloned.1.call-update) | async-done | bytes 6291472 | tf_op jit(solution)/shard_map/all_gather | solution.py:82
  91.2 0.0 copy-done
  91.2 20.1 %fusion.2 = (f32[4,16,64]{2,1,0:T(8,128)S(1)}, f32[4,3072,64,16]{1,2,3,0:T(8,128)}) fusion(pred[64,3072]{1,0:T(8,128)(4,1)S(1)} %compare_or_fusion, bf16[64,4,16,128]{3,2,1,0:T(8,128)(2,1)S(1)} %bitcast.69, bf16[3072,4,2,128]{3,0,1,2:T(8,128)(2,1)} %all-gather.2.cloned.1.call-done), kind=kOutput, calls=%fused_computation.4 | convolution fusion | flops 3258970112 | bytes 54738944 | tf_op jit(solution)/shard_map/tgqd,kgd->gqtk/dot_general | solution.py:42
  111.4 21.7 %fusion = f32[4,16,64]{2,1,0:T(8,128)S(1)} fusion(f32[4,3072,64,16]{1,2,3,0:T(8,128)} %get-tuple-element.10, f32[4,16,64]{2,1,0:T(8,128)S(1)} %compare_select_fusion, pred[64,3072]{1,0:T(8,128)(4,1)S(1)} %compare_or_fusion), kind=kLoop, calls=%fused_computation.2 | loop fusion | flops 50327552 | bytes 50561024 | tf_op jit(solution)/shard_map/reduce_sum | solution.py:48
  133.1 19.8 %fusion.14 = bf16[4,16,64,128]{3,2,1,0:T(8,128)(2,1)S(1)} fusion(bf16[3072,4,2,128]{3,0,1,2:T(8,128)(2,1)} %all-gather.2.cloned.1.call-done, f32[4,3072,64,16]{1,2,3,0:T(8,128)} %get-tuple-element.10, f32[4,16,64]{2,1,0:T(8,128)S(1)} %compare_select_fusion, pred[64,3072]{1,0:T(8,128)(4,1)S(1)} %compare_or_fusion, f32[4,16,64]{2,1,0:T(8,128)S(1)} %get-tuple-element.6, ...), kind=kOutput, calls=%fused_computation.13 | convolution fusion | flops 3407806464 | bytes 54828032 | tf_op jit(solution)/shard_map/dot_general | solution.py:92
  152.9 0.7 copy.21
  153.5 3.3 %collective-permute-start = (bf16[1,64,64,128]{3,2,1,0:T(8,128)(2,1)S(1)}, bf16[1,64,64,128]{3,2,1,0:T(8,128)(2,1)S(1)}, u32[]{:S(2)}, u32[]{:S(2)}) collective-permute-start(bf16[1,64,64,128]{3,2,1,0:T(8,128)(2,1)S(1)} %copy.21), channel_id=1, source_target_pairs={{0,64},{64,128},{128,192},{192,256},{256,320},{320,384},{384,448},... | collective-permute-start | bytes 3145736 | tf_op jit(solution)/shard_map/ppermute | solution.py:12
  156.8 25.6 %collective-permute-done = bf16[1,64,64,128]{3,2,1,0:T(8,128)(2,1)S(1)} collective-permute-done((bf16[1,64,64,128]{3,2,1,0:T(8,128)(2,1)S(1)}, bf16[1,64,64,128]{3,2,1,0:T(8,128)(2,1)S(1)}, u32[]{:S(2)}, u32[]{:S(2)}) %collective-permute-start) | collective-permute-done | bytes 1048608 | tf_op jit(solution)/shard_map/ppermute | solution.py:12
  182.4 1.0 copy.36
  (14 shorter events, 0.1 us)
Async XLA Ops:
  6.5 84.7 %copy-start = (bf16[1,64,64,128]{3,2,1,0:T(8,128)(2,1)S(1)}, bf16[1,64,64,128]{3,2,1,0:T(8,128)(2,1)}, u32[]{:S(2)}) copy-start(bf16[1,64,64,128]{3,2,1,0:T(8,128)(2,1)} %param.7) | copy-start | bytes 3145732
  6.5 84.7 %all-gather.2.cloned.1.call-start = ((), (), s32[]{:S(2)}) async-start(), calls=%async_computation | async-start | bytes 6488064 | tf_op jit(solution)/shard_map/all_gather | solution.py:82
  153.5 28.8 %collective-permute-start = (bf16[1,64,64,128]{3,2,1,0:T(8,128)(2,1)S(1)}, bf16[1,64,64,128]{3,2,1,0:T(8,128)(2,1)S(1)}, u32[]{:S(2)}, u32[]{:S(2)}) collective-permute-start(bf16[1,64,64,128]{3,2,1,0:T(8,128)(2,1)S(1)} %copy.21), channel_id=1, source_target_pairs={{0,64},{64,128},{128,192},{192,256},{256,320},{320,384},{384,448},... | collective-permute-start | bytes 3145736 | tf_op jit(solution)/shard_map/ppermute | solution.py:12
Sparse Core Ops, SparseCore 0:
  11.1 80.1 all-gather.1
where the time goes:
time: 191 us; the launch traced here: 190 us
  waiting for transfers between devices  104 us (54%)
  matrix products  39.9 us (21%)
  other arithmetic  26 us (14%)
  between operations  13.5 us (7%)
  local copies, waits for them, and re-layouts  3.63 us (2%)
  starting transfers between devices  3.28 us (2%)
    all_gather x1, waiting for transfers between devices, on_device(): lax.all_gather(own_block, 'ctx', axis=0, tiled=True)  78.2 us
    ppermute x1, waiting for transfers between devices, shifted(): return lax.ppermute(value, axis, pairs)  25.6 us
    reduce_sum x1, other arithmetic, attend(): total = total * rescale + jnp.sum(expo, axis=-1)  21.7 us
    dot_general x1, matrix products, attend(): jnp.einsum('tgqd,kgd->gqtk', grouped, keys, preferred_element_type=jnp.fl...  20.1 us
    dot_general x1, matrix products, on_device(): rotated = jnp.dot(mixed.reshape(-1, width), hadamard(width))  19.8 us
  transfers between devices with their start and end apart: 2, of which 2 were waited for; matrix products, arithmetic and copies ran while one was open for 1% of the time, Pallas kernels for 0%

commit v1 on v0

--- a/solution.py
+++ b/solution.py
@@ -79,7 +79,9 @@
     )
     carry = attend(
         initial,
-        lax.all_gather(own_block, "ctx", axis=0, tiled=True),
+        jnp.concatenate(
+            lax.all_to_all(jnp.stack([own_block] * lax.axis_size("ctx")), "ctx", 0, 0), axis=0
+        ),
         grouped,
         pos_query,
         order,

time: 191 us -> 263 us (1.38)
  waiting for transfers between devices: 104 us -> 166 us
  between operations: 13.5 us -> 0.16 us
  starting transfers between devices: 3.28 us -> 15 us
  local copies, waits for them, and re-layouts: 3.63 us -> 13 us
    all_to_all x0 -> x1, waiting for transfers between devices: none -> 139 us  [on_device(): lax.all_to_all(jnp.stack([own_block] * lax.axis_size('ctx')), 'ctx', 0, 0)]
    all_gather x1 -> x0, waiting for transfers between devices: 78.2 us -> none  [on_device(): lax.all_gather(own_block, 'ctx', axis=0, tiled=True)]
    all_to_all x0 -> x1, starting transfers between devices: none -> 11.3 us  [on_device(): lax.all_to_all(jnp.stack([own_block] * lax.axis_size('ctx')), 'ctx', 0, 0)]
    all_to_all x0 -> x1, local copies, waits for them, and re-layouts: none -> 6.68 us  [on_device(): lax.all_to_all(jnp.stack([own_block] * lax.axis_size('ctx')), 'ctx', 0, 0)]
    another operation x0 -> x2, local copies, waits for them, and re-layouts: none -> 4.22 us  [the longest x1 4.19 us: on_device(): jnp.stack([own_block] * lax.axis_size('ctx'))]
where the time goes in v1:
time: 263 us; the launch traced here: 261 us
  waiting for transfers between devices  166 us (63%)
  matrix products  39.9 us (15%)
  other arithmetic  27.4 us (10%)
  starting transfers between devices  15 us (6%)
  local copies, waits for them, and re-layouts  13 us (5%)
    all_to_all x1, waiting for transfers between devices, on_device(): lax.all_to_all(jnp.stack([own_block] * lax.axis_size('ctx')), 'ctx', 0, 0)  139 us
    ppermute x1, waiting for transfers between devices, shifted(): return lax.ppermute(value, axis, pairs)  26.9 us
    reduce_sum x1, other arithmetic, attend(): total = total * rescale + jnp.sum(expo, axis=-1)  21.7 us
    dot_general x1, matrix products, attend(): jnp.einsum('tgqd,kgd->gqtk', grouped, keys, preferred_element_type=jnp.fl...  20.2 us
    dot_general x1, matrix products, on_device(): rotated = jnp.dot(mixed.reshape(-1, width), hadamard(width))  19.8 us
    all_to_all x1, starting transfers between devices, on_device(): lax.all_to_all(jnp.stack([own_block] * lax.axis_size('ctx')), 'ctx', 0, 0)  11.3 us
    all_to_all x1, local copies, waits for them, and re-layouts, on_device(): lax.all_to_all(jnp.stack([own_block] * lax.axis_size('ctx')), 'ctx', 0, 0)  6.68 us
  transfers between devices with their start and end apart: 2, of which 2 were waited for; matrix products, arithmetic and copies ran while one was open for 1% of the time, Pallas kernels for 0%

profile of v1, /device:TPU:1, one launch (start us, length us, event | category | flops | bytes accessed | tf_op | source)
XLA Modules:
  0.0 261.3 jit_solution(14891874289135089742)
XLA Ops:
  0.0 0.0 copy-start
  0.0 0.8 exponential_bitcast_fusion
  0.8 0.1 copy.21
  0.9 0.1 broadcast_in_dim.66
  1.0 0.1 reshape.268
  1.1 0.1 copy.22
  1.1 0.1 copy.23
  1.2 0.9 fusion.30
  2.1 0.9 fusion.29
  3.0 1.0 maximum_bitcast_fusion
  4.0 0.1 pad_maximum_fusion
  4.2 4.2 %stack.11 = bf16[32,96,4,2,128]{4,1,2,3,0:T(8,128)(2,1)} broadcast(bf16[96,4,2,128]{3,0,1,2:T(8,128)(2,1)S(1)} %copy.24), dimensions={1,2,3,4} | broadcast | bytes 6488064 | tf_op jit(solution)/shard_map/stack | solution.py:83
  8.3 11.3 %all-to-all-start = ((bf16[32,96,4,2,128]{4,1,2,3,0:T(8,128)(2,1)}), bf16[32,96,4,2,128]{4,1,2,3,0:T(8,128)(2,1)}, u32[]{:S(2)}, u32[]{:S(2)}) async-start(bf16[32,96,4,2,128]{4,1,2,3,0:T(8,128)(2,1)} %stack.11), calls=%async_computation | async-start | bytes 12582912 | tf_op jit(solution)/shard_map/all_to_all | solution.py:83
  19.8 0.8 select_reduce_fusion.1
  20.6 0.9 select_reduce_fusion
  21.5 0.2 compare_or_fusion
  21.7 138.9 %all-to-all-done = bf16[32,96,4,2,128]{4,1,2,3,0:T(8,128)(2,1)} async-done(((bf16[32,96,4,2,128]{4,1,2,3,0:T(8,128)(2,1)}), bf16[32,96,4,2,128]{4,1,2,3,0:T(8,128)(2,1)}, u32[]{:S(2)}, u32[]{:S(2)}) %all-to-all-start) | async-done | bytes 6291488 | tf_op jit(solution)/shard_map/all_to_all | solution.py:83
  160.6 6.7 %copy.25 = bf16[32,96,4,2,128]{4,1,0,2,3:T(8,128)(2,1)} copy(bf16[32,96,4,2,128]{4,1,2,3,0:T(8,128)(2,1)} %all-to-all-done) | data formatting | bytes 12582912 | tf_op jit(solution)/shard_map/all_to_all | solution.py:83
  167.3 0.0 copy-done
  167.3 20.2 %fusion.2 = (f32[4,16,64]{2,1,0:T(8,128)S(1)}, f32[4,3072,64,16]{1,2,3,0:T(8,128)}) fusion(pred[64,3072]{1,0:T(8,128)(4,1)S(1)} %compare_or_fusion, bf16[64,4,16,128]{3,2,1,0:T(8,128)(2,1)S(1)} %bitcast.66, bf16[3072,4,2,128]{3,0,1,2:T(8,128)(2,1)} %bitcast.67), kind=kOutput, calls=%fused_computation.4 | convolution fusion | flops 3258970112 | bytes 54738944 | tf_op jit(solution)/shard_map/tgqd,kgd->gqtk/dot_general | solution.py:42
  187.5 0.0 copy-start.1
  187.5 21.7 %fusion = f32[4,16,64]{2,1,0:T(8,128)S(1)} fusion(f32[4,3072,64,16]{1,2,3,0:T(8,128)} %get-tuple-element.10, f32[4,16,64]{2,1,0:T(8,128)S(1)} %compare_select_fusion, pred[64,3072]{1,0:T(8,128)(4,1)S(1)} %compare_or_fusion), kind=kLoop, calls=%fused_computation.2 | loop fusion | flops 50327552 | bytes 50561024 | tf_op jit(solution)/shard_map/reduce_sum | solution.py:48
  209.3 19.8 %fusion.14 = bf16[4,16,64,128]{3,2,1,0:T(8,128)(2,1)S(1)} fusion(bf16[3072,4,2,128]{3,0,1,2:T(8,128)(2,1)} %bitcast.68, f32[4,3072,64,16]{1,2,3,0:T(8,128)} %get-tuple-element.10, f32[4,16,64]{2,1,0:T(8,128)S(1)} %compare_select_fusion, pred[64,3072]{1,0:T(8,128)(4,1)S(1)} %compare_or_fusion, f32[4,16,64]{2,1,0:T(8,128)S(1)} %get-tuple-element.6, ...), kind=kOutput, calls=%fused_computation.13 | convolution fusion | flops 3407806464 | bytes 54828032 | tf_op jit(solution)/shard_map/dot_general | solution.py:94
  229.1 0.7 copy.27
  229.7 3.6 %collective-permute-start = (bf16[1,64,64,128]{3,2,1,0:T(8,128)(2,1)S(1)}, bf16[1,64,64,128]{3,2,1,0:T(8,128)(2,1)S(1)}, u32[]{:S(2)}, u32[]{:S(2)}) collective-permute-start(bf16[1,64,64,128]{3,2,1,0:T(8,128)(2,1)S(1)} %copy.27), channel_id=1, source_target_pairs={{0,64},{64,128},{128,192},{192,256},{256,320},{320,384},{384,448},... | collective-permute-start | bytes 3145736 | tf_op jit(solution)/shard_map/ppermute | solution.py:12
  233.4 26.9 %collective-permute-done = bf16[1,64,64,128]{3,2,1,0:T(8,128)(2,1)S(1)} collective-permute-done((bf16[1,64,64,128]{3,2,1,0:T(8,128)(2,1)S(1)}, bf16[1,64,64,128]{3,2,1,0:T(8,128)(2,1)S(1)}, u32[]{:S(2)}, u32[]{:S(2)}) %collective-permute-start) | collective-permute-done | bytes 1048608 | tf_op jit(solution)/shard_map/ppermute | solution.py:12
  260.3 1.0 copy.36
  261.3 0.0 copy-done.1
  (13 shorter events, 0.1 us)
Async XLA Ops:
  0.0 167.3 %copy-start = (bf16[1,64,64,128]{3,2,1,0:T(8,128)(2,1)S(1)}, bf16[1,64,64,128]{3,2,1,0:T(8,128)(2,1)}, u32[]{:S(2)}) copy-start(bf16[1,64,64,128]{3,2,1,0:T(8,128)(2,1)} %param.7) | copy-start | bytes 3145732
  8.3 152.3 %all-to-all-start = ((bf16[32,96,4,2,128]{4,1,2,3,0:T(8,128)(2,1)}), bf16[32,96,4,2,128]{4,1,2,3,0:T(8,128)(2,1)}, u32[]{:S(2)}, u32[]{:S(2)}) async-start(bf16[32,96,4,2,128]{4,1,2,3,0:T(8,128)(2,1)} %stack.11), calls=%async_computation | async-start | bytes 12582912 | tf_op jit(solution)/shard_map/all_to_all | solution.py:83
  187.5 73.8 %copy-start.1 = (bf16[1,64,64,128]{3,2,1,0:T(8,128)(2,1)S(1)}, bf16[1,64,64,128]{3,2,1,0:T(8,128)(2,1)}, u32[]{:S(2)}) copy-start(bf16[1,64,64,128]{3,2,1,0:T(8,128)(2,1)} %param.7) | copy-start | bytes 3145732
  229.7 30.6 %collective-permute-start = (bf16[1,64,64,128]{3,2,1,0:T(8,128)(2,1)S(1)}, bf16[1,64,64,128]{3,2,1,0:T(8,128)(2,1)S(1)}, u32[]{:S(2)}, u32[]{:S(2)}) collective-permute-start(bf16[1,64,64,128]{3,2,1,0:T(8,128)(2,1)S(1)} %copy.27), channel_id=1, source_target_pairs={{0,64},{64,128},{128,192},{192,256},{256,320},{320,384},{384,448},... | collective-permute-start | bytes 3145736 | tf_op jit(solution)/shard_map/ppermute | solution.py:12
